TPU v7x, 32 devices: a whole 2x2x4 slice. The times are simulated.
32 devices in a mesh: row: 8 (over z, x), col: 4 (over y, core).
Axes of the slice: x: 2, y: 2, z: 4, core: 2. Of those that a mesh axis runs over, the one named last changes fastest.
Arguments:
- vectors: bfloat16 [4, 4, 8, 16, 256], P(None, 'col', 'row'), may hold values from -6 to 6
- tiles: bfloat16 [8, 4, 64, 256, 256], P('row', 'col'), may hold values from -0.0625 to 0.0625
- tile_coords: int32 [8, 4, 64, 2], P('row', 'col'), may hold values from 0 to 127, as said below
- tile_count: int32 [8, 4], P('row', 'col'), may hold values from 16 to 64, as said below
Outputs:
- product: float32 [4, 4, 8, 16, 256], P(None, 'col', 'row')
Inputs may be any that keep to these rules, and one draw needn't show every extreme that they name: `tile_coords`: for the device in grid row r and grid column c every slot's block row I has I % 8 == r, its block column J has (J // 8) % 4 == c, and J <= I. `tile_count`: counts differ from device to device; in every draw some device uses all 64 slots and some other uses 64 // 4.
All inputs are finite; a program needn't handle non-finite values.
Results may differ from a plain program's by a relative error of at most 0.0003.
Values may be sent and summed in bfloat16 or wider, within the bound.
No kernel may reach another device: no remote copies, remote signals or barrier semaphores. Data moves between devices by JAX's collectives and lax.ppermute only.
A program may use at most 64 MiB of HBM per device.

v0:
```python
import functools

import jax
import jax.numpy as jnp
from jax import lax
from jax.experimental import pallas as pl
from jax.experimental.pallas import tpu as pltpu
from jax.sharding import PartitionSpec as P


GROUP = 16
LEVELS = 32000.0
TINY = 1e-30
ROWS_MIN = 8


def extra_rows(repeats):
    return -(-repeats // ROWS_MIN) * ROWS_MIN


def encode(blocks, out):
    repeats = len(blocks)
    vec, width = blocks[0].shape
    tail = extra_rows(repeats)
    row = lax.broadcasted_iota(jnp.int32, (tail, width), 0)
    exponents = jnp.zeros((tail, width), jnp.float32)
    for k, block in enumerate(blocks):
        top = jnp.max(jnp.abs(block), axis=0, keepdims=True)
        exponent = jnp.ceil(jnp.log2(jnp.maximum(top, TINY)))
        coded = block * jnp.exp2(-exponent) * LEVELS
        out[k * vec : (k + 1) * vec, :] = jnp.round(coded).astype(jnp.int32).astype(jnp.int16)
        exponents = jnp.where(row == k, exponent, exponents)
    out[repeats * vec :, :] = exponents.astype(jnp.int32).astype(jnp.int16)


def decode(coded, repeats, vec):
    tail = coded[repeats * vec :, :].astype(jnp.int32).astype(jnp.float32)
    scales = jnp.exp2(tail) * (1.0 / LEVELS)
    return [
        coded[k * vec : (k + 1) * vec, :].astype(jnp.int32).astype(jnp.float32) * scales[k : k + 1, :]
        for k in range(repeats)
    ]


def mirrored_bits(value, n):
    bits = n.bit_length() - 1
    turned = 0
    for i in range(bits):
        turned += ((value >> i) & 1) << (bits - 1 - i)
    return turned


def places(coords, s, rows, cols, repeats):
    upper, lower = coords[0, s], coords[1, s]
    cells = rows * cols
    own_row = lax.rem(upper, rows)
    own_col = lax.rem(lax.div(lower, rows), cols)
    upper_col = lax.div(lax.rem(upper, cells), rows)
    away = lax.rem(lower, rows) ^ own_row
    upper_at = (upper_col ^ own_col) * repeats + lax.div(upper, cells)
    lower_out = away * repeats + lax.div(lower, cells)
    lower_at = mirrored_bits(away, rows) * repeats + lax.div(lower, cells)
    return upper_at, lower_out, lower_at


def multiply(count, tiles, held, total, at, contracted):
    filled = count[0]
    total[...] = jnp.zeros_like(total)

    def turn(g, carry):
        for q in range(GROUP):
            s = g * GROUP + q
            source, target = at(s)
            x = held[source]
            x = jnp.where(s < filled, x, jnp.zeros_like(x))
            total[target] += lax.dot_general(
                x, tiles[s], (((1,), (contracted,)), ((), ())), preferred_element_type=jnp.float32
            )
        return carry

    lax.fori_loop(0, lax.div(filled + GROUP - 1, GROUP), turn, 0)


def load_pieces(pieces, held):
    at = 0
    for piece in pieces:
        count = piece.shape[0]
        held[at : at + count] = piece[...]
        at += count


def mirror_kernel(rows, cols, repeats, away, count, coords, tiles, *refs):
    *pieces, total, coded, held = refs
    load_pieces(pieces, held)

    def at(s):
        upper_at, lower_out, _ = places(coords, s, rows, cols, repeats)
        return upper_at, lower_out

    multiply(count, tiles, held, total, at, 0)
    for i, o in enumerate(away):
        encode([total[o * repeats + k] for k in range(repeats)], coded.at[i])


def forward_kernel(rows, cols, repeats, count, coords, tiles, *refs):
    *refs, held, total = refs
    pieces, outs = refs[:-cols], refs[-cols:]
    load_pieces(pieces, held)

    def at(s):
        upper_at, _, lower_at = places(coords, s, rows, cols, repeats)
        return lower_at, upper_at

    multiply(count, tiles, held, total, at, 1)
    outs[0][...] = total[0:repeats]
    for o in range(1, cols):
        encode([total[o * repeats + k] for k in range(repeats)], outs[o])


def fold_kernel(repeats, vec, kept, away, total, received, *outs):
    kept_out, coded = outs
    for i, o in enumerate(kept):
        sums = decode(received.at[i], repeats, vec)
        sums = [total[o * repeats + k] + sums[k] for k in range(repeats)]
        if i in away:
            encode(sums, coded.at[away.index(i)])
        else:
            at = [j for j in range(len(kept)) if j not in away].index(i)
            for k in range(repeats):
                kept_out[at * repeats + k] = sums[k]


def final_kernel(repeats, own_rows, own_cols, *refs):
    *received, out = refs
    vec = own_rows.shape[1]
    sums = [own_rows[k] + own_cols[k] for k in range(repeats)]
    for ref in received:
        sums = [a + b for a, b in zip(sums, decode(ref, repeats, vec))]
    for k in range(repeats):
        out[k] = sums[k]


def anchor_kernel(out):
    out[...] = jnp.zeros_like(out)


def prepare_kernel(anchor, vectors_far, vectors, arrived):
    copy = pltpu.make_async_copy(vectors_far, vectors, arrived)
    copy.start()
    copy.wait()


def halving(n):
    bits = [1 << i for i in reversed(range(n.bit_length() - 1))]
    return bits[1:] + bits[:1]


def partners(n, offset):
    return [(i, i ^ offset) for i in range(n)]


def body(vectors, tiles, tile_coords, tile_count):
    rows, cols = lax.axis_size("row"), lax.axis_size("col")
    repeats, vec, width = vectors.shape[0], vectors.shape[3], vectors.shape[4]
    slots = tiles.shape[2]
    if rows & (rows - 1) or cols & (cols - 1) or slots % GROUP:
        raise ValueError("sizes")
    mine = vectors.reshape(repeats, vec, width)
    mats = tiles.reshape(slots, width, width)
    coords = tile_coords.reshape(slots, 2).T
    coded_rows = repeats * vec + extra_rows(repeats)

    vmem = pl.BlockSpec(memory_space=pltpu.VMEM)
    far = pl.BlockSpec(memory_space=pl.ANY)
    anchor = pl.pallas_call(
        anchor_kernel,
        out_shape=jax.ShapeDtypeStruct((8, 128), jnp.float32),
        out_specs=vmem,
        compiler_params=pltpu.CompilerParams(vmem_limit_bytes=1 << 20),
        cost_estimate=pl.CostEstimate(flops=1 << 36, bytes_accessed=1 << 10, transcendentals=0),
        name="anchor",
    )()
    near = pl.pallas_call(
        prepare_kernel,
        out_shape=jax.ShapeDtypeStruct(mine.shape, mine.dtype),
        in_specs=[vmem, far],
        out_specs=vmem,
        scratch_shapes=[pltpu.SemaphoreType.DMA],
        compiler_params=pltpu.CompilerParams(vmem_limit_bytes=2 << 20),
        cost_estimate=pl.CostEstimate(flops=0, bytes_accessed=1 << 20, transcendentals=0),
        name="prepare",
    )(anchor, mine)
    filled = tile_count.reshape(1)

    pieces, offsets = [mine], [0]
    bit = cols // 2
    while bit:
        moved = []
        for piece in pieces:
            moved.append(lax.ppermute(piece, "col", partners(cols, bit)))
        pieces += moved
        offsets += [o ^ bit for o in offsets]
        bit //= 2
    pieces[0] = near
    row_pieces = [piece for _, piece in sorted(zip(offsets, pieces), key=lambda pair: pair[0])]

    column_pieces = [near]
    bit = rows // 2
    while bit:
        held = jnp.concatenate(column_pieces, axis=0) if bit < rows // 2 else mine
        column_pieces.append(lax.ppermute(held, "row", partners(rows, bit)))
        bit //= 2

    smem = pl.BlockSpec(memory_space=pltpu.SMEM)
    params = pltpu.CompilerParams(vmem_limit_bytes=16 << 20)
    cost = pl.CostEstimate(
        flops=2 * slots * vec * width * width, bytes_accessed=2 * slots * width * width, transcendentals=0
    )
    small = pl.CostEstimate(flops=0, bytes_accessed=1 << 20, transcendentals=0)

    def coded(n):
        return jax.ShapeDtypeStruct((n, coded_rows, width), jnp.int16)

    def blocks(n):
        return jax.ShapeDtypeStruct((n * repeats, vec, width), jnp.float32)

    order = halving(rows)
    held = list(range(rows))
    away = [o for o in held if o & order[0]]
    total, sent = pl.pallas_call(
        functools.partial(mirror_kernel, rows, cols, repeats, away),
        out_shape=[blocks(rows), coded(len(away))],
        in_specs=[smem, smem] + [vmem] * (1 + cols),
        out_specs=[vmem, vmem],
        scratch_shapes=[pltpu.VMEM((cols * repeats, vec, width), jnp.bfloat16)],
        compiler_params=params,
        cost_estimate=cost,
        name="mirror",
    )(filled, coords, mats, *row_pieces)
    for step, bit in enumerate(order):
        received = lax.ppermute(sent, "row", partners(rows, bit))
        if step == len(order) - 1:
            break
        stay = [i for i, o in enumerate(held) if not o & bit]
        left = [held[i] for i in stay]
        following = order[step + 1]
        go = [i for i, o in enumerate(left) if o & following]
        total, sent = pl.pallas_call(
            functools.partial(fold_kernel, repeats, vec, stay, go),
            out_shape=[blocks(len(left) - len(go)), coded(len(go))],
            in_specs=[vmem, vmem],
            out_specs=[vmem, vmem],
            compiler_params=params,
            cost_estimate=small,
        )(total, received)
        held = [o for o in left if not o & following]

    own, *partial = pl.pallas_call(
        functools.partial(forward_kernel, rows, cols, repeats),
        out_shape=[blocks(1)] + [jax.ShapeDtypeStruct((coded_rows, width), jnp.int16)] * (cols - 1),
        in_specs=[smem, smem] + [vmem] * (1 + len(column_pieces)),
        out_specs=[vmem] * cols,
        scratch_shapes=[
            pltpu.VMEM((rows * repeats, vec, width), jnp.bfloat16),
            pltpu.VMEM((cols * repeats, vec, width), jnp.float32),
        ],
        compiler_params=params,
        cost_estimate=cost,
        name="forward",
    )(filled, coords, mats, *column_pieces)
    gathered = []
    for o, part in enumerate(partial):
        gathered.append(lax.ppermute(part, "col", partners(cols, o + 1)))

    out = pl.pallas_call(
        functools.partial(final_kernel, repeats),
        out_shape=blocks(1),
        in_specs=[vmem] * (2 + cols),
        out_specs=vmem,
        compiler_params=params,
        name="final",
    )(total, own, received.reshape(coded_rows, width), *gathered)
    return out.reshape(repeats, 1, 1, vec, width)


def solution(mesh):
    return jax.shard_map(
        body,
        mesh=mesh,
        in_specs=(
            P(None, "col", "row", None, None),
            P("row", "col", None, None, None),
            P("row", "col", None, None),
            P("row", "col"),
        ),
        out_specs=P(None, "col", "row", None, None),
        check_vma=False,
    )
```

profile of v0, /device:TPU:0, one launch (start us, length us, event | category | flops | bytes accessed | tf_op | source)
XLA Modules:
  0.0 32.1 jit_solution(8254503077209240919)
XLA Ops:
  0.0 3.1 %collective-permute-start.1 = (bf16[4,16,256]{2,1,0:T(8,128)(2,1)}, bf16[4,16,256]{2,1,0:T(8,128)(2,1)S(1)}, u32[]{:S(2)}, u32[]{:S(2)}) collective-permute-start(bf16[4,16,256]{2,1,0:T(8,128)(2,1)} %bitcast.17), channel_id=1, source_target_pairs={{0,2},{1,3},{2,0},{3,1},{4,6},{5,7},{6,4},{7,5},{8,10},{9,11},{10,... | collective-permute-start | bytes 98312 | tf_op jit(solution)/shard_map/ppermute | solution.py:200
  3.1 2.6 %collective-permute-start.5 = (bf16[4,16,256]{2,1,0:T(8,128)(2,1)}, bf16[4,16,256]{2,1,0:T(8,128)(2,1)S(1)}, u32[]{:S(2)}, u32[]{:S(2)}) collective-permute-start(bf16[4,16,256]{2,1,0:T(8,128)(2,1)} %bitcast.18), channel_id=1, source_target_pairs={{0,16},{4,20},{8,24},{12,28},{16,0},{20,4},{24,8},{28,12},{1,17},{... | collective-permute-start | bytes 98312 | tf_op jit(solution)/shard_map/ppermute | solution.py:211
  5.7 0.0 copy-done
  5.7 2.4 %collective-permute-done.5.refs_1_ = bf16[4,16,256]{2,1,0:T(8,128)(2,1)S(1)} collective-permute-done((bf16[4,16,256]{2,1,0:T(8,128)(2,1)}, bf16[4,16,256]{2,1,0:T(8,128)(2,1)S(1)}, u32[]{:S(2)}, u32[]{:S(2)}) %collective-permute-start.5) | collective-permute-done | bytes 32800 | tf_op jit(solution)/shard_map/ppermute | solution.py:211
  8.1 1.6 %collective-permute-start.6 = (bf16[8,16,256]{2,1,0:T(8,128)(2,1)S(1)}, bf16[8,16,256]{2,1,0:T(8,128)(2,1)S(1)}, u32[]{:S(2)}, u32[]{:S(2)}) collective-permute-start(bf16[8,16,256]{2,1,0:T(8,128)(2,1)S(1)} %pad_maximum_fusion.1), channel_id=1, source_target_pairs={{0,8},{4,12},{8,0},{12,4},{16,24},{20,28},{24,16},{28,20},{1,9},{5... | collective-permute-start | bytes 196616 | tf_op jit(solution)/shard_map/ppermute | solution.py:211
  9.8 0.0 collective-permute-start
  9.8 0.0 collective-permute-done.1.refs_2_
  9.8 0.5 %collective-permute-start.2 = (bf16[4,16,256]{2,1,0:T(8,128)(2,1)S(1)}, bf16[4,16,256]{2,1,0:T(8,128)(2,1)S(1)}, u32[]{:S(2)}, u32[]{:S(2)}) collective-permute-start(bf16[4,16,256]{2,1,0:T(8,128)(2,1)S(1)} %collective-permute-done.1.refs_2_), channel_id=1, source_target_pairs={{0,1},{1,0},{2,3},{3,2},{4,5},{5,4},{6,7},{7,6},{8,9},{9,8},{10,11... | collective-permute-start | bytes 98312 | tf_op jit(solution)/shard_map/ppermute | solution.py:200
  10.9 0.0 collective-permute-done.refs_1_
  11.0 0.2 collective-permute-done.2.refs_3_
  11.1 0.0 slice-done
  11.1 0.0 slice-done.1
  11.1 1.6 %mirror.1 = (f32[32,16,256]{2,1,0:T(8,128)S(1)}, s16[4,72,256]{2,1,0:T(8,128)(2,1)S(1)}) custom-call(s32[1]{0:T(128)} %bitcast.10.count, s32[2,64]{1,0:T(2,128)S(1)} %bitcast.21, bf16[64,256,256]{2,1,0:T(8,128)(2,1)S(1)} %bitcast.14, bf16[4,16,256]{2,1,0:T(8,128)(2,1)S(1)} %prepare.1.refs_0_, bf16[4,16,256]{2,1,0:T(8,128)(2,1)S(1)} %collective-permute-done.refs_1_, ...), custom_call_target="tpu_custom_call" | custom-call | flops 134217728 | bytes 8388608 | tf_op jit(solution)/shard_map/mirror/pallas_call | solution.py:230
  12.7 0.5 %collective-permute-start.3 = (s16[4,72,256]{2,1,0:T(8,128)(2,1)S(1)}, s16[4,72,256]{2,1,0:T(8,128)(2,1)S(1)}, u32[]{:S(2)}, u32[]{:S(2)}) collective-permute-start(s16[4,72,256]{2,1,0:T(8,128)(2,1)S(1)} %get-tuple-element.16), channel_id=1, source_target_pairs={{0,8},{4,12},{8,0},{12,4},{16,24},{20,28},{24,16},{28,20},{1,9},{5... | collective-permute-start | bytes 442376 | tf_op jit(solution)/shard_map/ppermute | solution.py:241
  13.2 0.0 collective-permute-done.6.refs_2_
  13.2 2.4 %collective-permute-start.7 = (bf16[16,16,256]{2,1,0:T(8,128)(2,1)S(1)}, bf16[16,16,256]{2,1,0:T(8,128)(2,1)S(1)}, u32[]{:S(2)}, u32[]{:S(2)}) collective-permute-start(bf16[16,16,256]{2,1,0:T(8,128)(2,1)S(1)} %pad_maximum_fusion), channel_id=1, source_target_pairs={{0,4},{4,0},{8,12},{12,8},{16,20},{20,16},{24,28},{28,24},{1,5},{5... | collective-permute-start | bytes 393224 | tf_op jit(solution)/shard_map/ppermute | solution.py:211
  15.6 3.6 %collective-permute-done.3.received = s16[4,72,256]{2,1,0:T(8,128)(2,1)S(1)} collective-permute-done((s16[4,72,256]{2,1,0:T(8,128)(2,1)S(1)}, s16[4,72,256]{2,1,0:T(8,128)(2,1)S(1)}, u32[]{:S(2)}, u32[]{:S(2)}) %collective-permute-start.3) | collective-permute-done | bytes 147488 | tf_op jit(solution)/shard_map/ppermute | solution.py:241
  19.3 0.1 shard_map.46
  19.4 1.6 %collective-permute-start.4 = (s16[2,72,256]{2,1,0:T(8,128)(2,1)S(1)}, s16[2,72,256]{2,1,0:T(8,128)(2,1)S(1)}, u32[]{:S(2)}, u32[]{:S(2)}) collective-permute-start(s16[2,72,256]{2,1,0:T(8,128)(2,1)S(1)} %get-tuple-element.18), channel_id=1, source_target_pairs={{0,4},{4,0},{8,12},{12,8},{16,20},{20,16},{24,28},{28,24},{1,5},{5... | collective-permute-start | bytes 221192 | tf_op jit(solution)/shard_map/ppermute | solution.py:241
  21.0 0.0 collective-permute-done.7.refs_3_
  21.0 2.0 %forward.1 = (f32[4,16,256]{2,1,0:T(8,128)S(1)}, s16[72,256]{1,0:T(8,128)(2,1)S(1)}, s16[72,256]{1,0:T(8,128)(2,1)S(1)}, s16[72,256]{1,0:T(8,128)(2,1)S(1)}) custom-call(s32[1]{0:T(128)} %bitcast.11.count, s32[2,64]{1,0:T(2,128)S(1)} %bitcast.22, bf16[64,256,256]{2,1,0:T(8,128)(2,1)S(1)} %bitcast.15, bf16[4,16,256]{2,1,0:T(8,128)(2,1)S(1)} %prepare.1.refs_0_, ...), custom_call_target="tpu_custom_call" | custom-call | flops 134217728 | bytes 8388608 | tf_op jit(solution)/shard_map/forward/pallas_call | solution.py:258
  23.0 1.2 %collective-permute-start.10 = (s16[72,256]{1,0:T(8,128)(2,1)S(1)}, s16[72,256]{1,0:T(8,128)(2,1)S(1)}, u32[]{:S(2)}, u32[]{:S(2)}) collective-permute-start(s16[72,256]{1,0:T(8,128)(2,1)S(1)} %get-tuple-element.23), channel_id=1, source_target_pairs={{0,2},{1,3},{2,0},{3,1},{4,6},{5,7},{6,4},{7,5},{8,10},{9,11},{10,... | collective-permute-start | bytes 110600 | tf_op jit(solution)/shard_map/ppermute | solution.py:273
  24.2 1.1 %collective-permute-start.11 = (s16[72,256]{1,0:T(8,128)(2,1)S(1)}, s16[72,256]{1,0:T(8,128)(2,1)S(1)}, u32[]{:S(2)}, u32[]{:S(2)}) collective-permute-start(s16[72,256]{1,0:T(8,128)(2,1)S(1)} %get-tuple-element.24), channel_id=1, source_target_pairs={{0,3},{1,2},{2,1},{3,0},{4,7},{5,6},{6,5},{7,4},{8,11},{9,10},{10,... | collective-permute-start | bytes 110600 | tf_op jit(solution)/shard_map/ppermute | solution.py:273
  25.3 0.0 collective-permute-start.9
  25.4 0.0 collective-permute-done.4.received
  25.4 0.1 shard_map.47
  25.4 4.0 %collective-permute-start.8 = (s16[1,72,256]{2,1,0:T(8,128)(2,1)S(1)}, s16[1,72,256]{2,1,0:T(8,128)(2,1)S(1)}, u32[]{:S(2)}, u32[]{:S(2)}) collective-permute-start(s16[1,72,256]{2,1,0:T(8,128)(2,1)S(1)} %get-tuple-element.21), channel_id=1, source_target_pairs={{0,16},{4,20},{8,24},{12,28},{16,0},{20,4},{24,8},{28,12},{1,17},{... | collective-permute-start | bytes 110600 | tf_op jit(solution)/shard_map/ppermute | solution.py:241
  29.4 0.0 collective-permute-done.10.refs_2_
  29.4 0.0 collective-permute-done.11.refs_3_
  29.4 0.0 collective-permute-done.9.refs_1_
  29.4 2.0 %collective-permute-done.8 = s16[1,72,256]{2,1,0:T(8,128)(2,1)S(1)} collective-permute-done((s16[1,72,256]{2,1,0:T(8,128)(2,1)S(1)}, s16[1,72,256]{2,1,0:T(8,128)(2,1)S(1)}, u32[]{:S(2)}, u32[]{:S(2)}) %collective-permute-start.8) | collective-permute-done | bytes 36896 | tf_op jit(solution)/shard_map/ppermute | solution.py:241
  31.5 0.7 %final.1 = f32[4,16,256]{2,1,0:T(8,128)} custom-call(f32[4,16,256]{2,1,0:T(8,128)S(1)} %get-tuple-element.19.own_rows, f32[4,16,256]{2,1,0:T(8,128)S(1)} %get-tuple-element.20.own_cols, s16[72,256]{1,0:T(8,128)(2,1)S(1)} %bitcast.16, s16[72,256]{1,0:T(8,128)(2,1)S(1)} %collective-permute-done.9.refs_1_, s16[72,256]{1,0:T(8,128)(2,1)S(1)} %collective-permute-done.10.refs_2_, ...), custom_call_target="tpu_custom_call" | custom-call | tf_op jit(solution)/shard_map/final/pallas_call | solution.py:275
  (10 shorter events, 0.1 us)
Async XLA Ops:
  0.0 11.1 %slice-start = ((s8[8388608]{0:T(1024)(128)(4,1)}), s8[4194304]{0:T(1024)(128)(4,1)S(1)}, s32[]{:S(2)}) async-start(s8[8388608]{0:T(1024)(128)(4,1)} %bitcast.12), calls=%async_computation | async-start | bytes 8388608
  0.0 5.7 %copy-start = (bf16[4,1,1,16,256]{4,3,2,1,0:T(8,128)(2,1)S(1)}, bf16[4,1,1,16,256]{4,3,2,1,0:T(8,128)(2,1)}, u32[]{:S(2)}) copy-start(bf16[4,1,1,16,256]{4,3,2,1,0:T(8,128)(2,1)} %param.4) | copy-start | bytes 98308
  0.0 11.1 %slice-start.1 = ((s8[8388608]{0:T(1024)(128)(4,1)}), s8[4194304]{0:T(1024)(128)(4,1)S(1)}, s32[]{:S(2)}) async-start(s8[8388608]{0:T(1024)(128)(4,1)} %bitcast.12), calls=%async_computation.1 | async-start | bytes 8388608
  0.0 11.1 %copy-start.1 = (s32[1,1,64,2]{2,3,1,0:T(2,128)S(1)}, s32[1,1,64,2]{2,3,1,0:T(2,128)}, u32[]{:S(2)}) copy-start(s32[1,1,64,2]{2,3,1,0:T(2,128)} %param.6) | copy-start | bytes 1540
  0.0 9.8 %collective-permute-start.1 = (bf16[4,16,256]{2,1,0:T(8,128)(2,1)}, bf16[4,16,256]{2,1,0:T(8,128)(2,1)S(1)}, u32[]{:S(2)}, u32[]{:S(2)}) collective-permute-start(bf16[4,16,256]{2,1,0:T(8,128)(2,1)} %bitcast.17), channel_id=1, source_target_pairs={{0,2},{1,3},{2,0},{3,1},{4,6},{5,7},{6,4},{7,5},{8,10},{9,11},{10,... | collective-permute-start | bytes 98312 | tf_op jit(solution)/shard_map/ppermute | solution.py:200
  3.1 5.0 %collective-permute-start.5 = (bf16[4,16,256]{2,1,0:T(8,128)(2,1)}, bf16[4,16,256]{2,1,0:T(8,128)(2,1)S(1)}, u32[]{:S(2)}, u32[]{:S(2)}) collective-permute-start(bf16[4,16,256]{2,1,0:T(8,128)(2,1)} %bitcast.18), channel_id=1, source_target_pairs={{0,16},{4,20},{8,24},{12,28},{16,0},{20,4},{24,8},{28,12},{1,17},{... | collective-permute-start | bytes 98312 | tf_op jit(solution)/shard_map/ppermute | solution.py:211
  8.1 5.1 %collective-permute-start.6 = (bf16[8,16,256]{2,1,0:T(8,128)(2,1)S(1)}, bf16[8,16,256]{2,1,0:T(8,128)(2,1)S(1)}, u32[]{:S(2)}, u32[]{:S(2)}) collective-permute-start(bf16[8,16,256]{2,1,0:T(8,128)(2,1)S(1)} %pad_maximum_fusion.1), channel_id=1, source_target_pairs={{0,8},{4,12},{8,0},{12,4},{16,24},{20,28},{24,16},{28,20},{1,9},{5... | collective-permute-start | bytes 196616 | tf_op jit(solution)/shard_map/ppermute | solution.py:211
  9.8 1.2 %collective-permute-start = (bf16[4,16,256]{2,1,0:T(8,128)(2,1)S(1)}, bf16[4,16,256]{2,1,0:T(8,128)(2,1)S(1)}, u32[]{:S(2)}, u32[]{:S(2)}) collective-permute-start(bf16[4,16,256]{2,1,0:T(8,128)(2,1)S(1)} %bitcast.20), channel_id=1, source_target_pairs={{0,1},{1,0},{2,3},{3,2},{4,5},{5,4},{6,7},{7,6},{8,9},{9,8},{10,11... | collective-permute-start | bytes 98312 | tf_op jit(solution)/shard_map/ppermute | solution.py:200
  9.8 1.4 %collective-permute-start.2 = (bf16[4,16,256]{2,1,0:T(8,128)(2,1)S(1)}, bf16[4,16,256]{2,1,0:T(8,128)(2,1)S(1)}, u32[]{:S(2)}, u32[]{:S(2)}) collective-permute-start(bf16[4,16,256]{2,1,0:T(8,128)(2,1)S(1)} %collective-permute-done.1.refs_2_), channel_id=1, source_target_pairs={{0,1},{1,0},{2,3},{3,2},{4,5},{5,4},{6,7},{7,6},{8,9},{9,8},{10,11... | collective-permute-start | bytes 98312 | tf_op jit(solution)/shard_map/ppermute | solution.py:200
  12.7 6.6 %collective-permute-start.3 = (s16[4,72,256]{2,1,0:T(8,128)(2,1)S(1)}, s16[4,72,256]{2,1,0:T(8,128)(2,1)S(1)}, u32[]{:S(2)}, u32[]{:S(2)}) collective-permute-start(s16[4,72,256]{2,1,0:T(8,128)(2,1)S(1)} %get-tuple-element.16), channel_id=1, source_target_pairs={{0,8},{4,12},{8,0},{12,4},{16,24},{20,28},{24,16},{28,20},{1,9},{5... | collective-permute-start | bytes 442376 | tf_op jit(solution)/shard_map/ppermute | solution.py:241
  13.2 7.7 %collective-permute-start.7 = (bf16[16,16,256]{2,1,0:T(8,128)(2,1)S(1)}, bf16[16,16,256]{2,1,0:T(8,128)(2,1)S(1)}, u32[]{:S(2)}, u32[]{:S(2)}) collective-permute-start(bf16[16,16,256]{2,1,0:T(8,128)(2,1)S(1)} %pad_maximum_fusion), channel_id=1, source_target_pairs={{0,4},{4,0},{8,12},{12,8},{16,20},{20,16},{24,28},{28,24},{1,5},{5... | collective-permute-start | bytes 393224 | tf_op jit(solution)/shard_map/ppermute | solution.py:211
  19.4 6.0 %collective-permute-start.4 = (s16[2,72,256]{2,1,0:T(8,128)(2,1)S(1)}, s16[2,72,256]{2,1,0:T(8,128)(2,1)S(1)}, u32[]{:S(2)}, u32[]{:S(2)}) collective-permute-start(s16[2,72,256]{2,1,0:T(8,128)(2,1)S(1)} %get-tuple-element.18), channel_id=1, source_target_pairs={{0,4},{4,0},{8,12},{12,8},{16,20},{20,16},{24,28},{28,24},{1,5},{5... | collective-permute-start | bytes 221192 | tf_op jit(solution)/shard_map/ppermute | solution.py:241
  23.0 6.5 %collective-permute-start.10 = (s16[72,256]{1,0:T(8,128)(2,1)S(1)}, s16[72,256]{1,0:T(8,128)(2,1)S(1)}, u32[]{:S(2)}, u32[]{:S(2)}) collective-permute-start(s16[72,256]{1,0:T(8,128)(2,1)S(1)} %get-tuple-element.23), channel_id=1, source_target_pairs={{0,2},{1,3},{2,0},{3,1},{4,6},{5,7},{6,4},{7,5},{8,10},{9,11},{10,... | collective-permute-start | bytes 110600 | tf_op jit(solution)/shard_map/ppermute | solution.py:273
  24.2 5.2 %collective-permute-start.11 = (s16[72,256]{1,0:T(8,128)(2,1)S(1)}, s16[72,256]{1,0:T(8,128)(2,1)S(1)}, u32[]{:S(2)}, u32[]{:S(2)}) collective-permute-start(s16[72,256]{1,0:T(8,128)(2,1)S(1)} %get-tuple-element.24), channel_id=1, source_target_pairs={{0,3},{1,2},{2,1},{3,0},{4,7},{5,6},{6,5},{7,4},{8,11},{9,10},{10,... | collective-permute-start | bytes 110600 | tf_op jit(solution)/shard_map/ppermute | solution.py:273
  25.3 4.1 %collective-permute-start.9 = (s16[72,256]{1,0:T(8,128)(2,1)S(1)}, s16[72,256]{1,0:T(8,128)(2,1)S(1)}, u32[]{:S(2)}, u32[]{:S(2)}) collective-permute-start(s16[72,256]{1,0:T(8,128)(2,1)S(1)} %get-tuple-element.22), channel_id=1, source_target_pairs={{0,1},{1,0},{2,3},{3,2},{4,5},{5,4},{6,7},{7,6},{8,9},{9,8},{10,11... | collective-permute-start | bytes 110600 | tf_op jit(solution)/shard_map/ppermute | solution.py:273
  25.4 6.0 %collective-permute-start.8 = (s16[1,72,256]{2,1,0:T(8,128)(2,1)S(1)}, s16[1,72,256]{2,1,0:T(8,128)(2,1)S(1)}, u32[]{:S(2)}, u32[]{:S(2)}) collective-permute-start(s16[1,72,256]{2,1,0:T(8,128)(2,1)S(1)} %get-tuple-element.21), channel_id=1, source_target_pairs={{0,16},{4,20},{8,24},{12,28},{16,0},{20,4},{24,8},{28,12},{1,17},{... | collective-permute-start | bytes 110600 | tf_op jit(solution)/shard_map/ppermute | solution.py:241
where the time goes:
time: 32.3 us; the launch traced here: 32.1 us
  starting transfers between devices  18.7 us (58%)
  waiting for transfers between devices  8.25 us (26%)
  Pallas kernels  4.44 us (14%)
  between operations  0.7 us (2%)
    ppermute x3, starting transfers between devices, body(): column_pieces.append(lax.ppermute(held, 'row', partners(rows, bit)))  6.63 us
    ppermute x3, starting transfers between devices, body(): received = lax.ppermute(sent, 'row', partners(rows, bit))  6.11 us
    ppermute x3, waiting for transfers between devices, body(): received = lax.ppermute(sent, 'row', partners(rows, bit))  5.64 us
    ppermute x3, starting transfers between devices, body(): moved.append(lax.ppermute(piece, 'col', partners(cols, bit)))  3.58 us
    ppermute x3, waiting for transfers between devices, body(): column_pieces.append(lax.ppermute(held, 'row', partners(rows, bit)))  2.39 us
    ppermute x3, starting transfers between devices, body(): gathered.append(lax.ppermute(part, 'col', partners(cols, o + 1)))  2.38 us
    pallas_call x1, Pallas kernels, body(): pl.pallas_call(functools.partial(forward_kernel, rows, cols, repeats), ou...  2 us
    pallas_call x1, Pallas kernels, body(): pl.pallas_call(functools.partial(mirror_kernel, rows, cols, repeats, away...  1.55 us
  transfers between devices with their start and end apart: 12, of which 4 were waited for; matrix products, arithmetic and copies ran while one was open for 0% of the time, Pallas kernels for 12%

commit v1 on v0

--- a/solution.py
+++ b/solution.py
@@ -50,35 +50,47 @@
     return turned
 
 
-def places(coords, s, rows, cols, repeats):
-    upper, lower = coords[0, s], coords[1, s]
-    cells = rows * cols
-    own_row = lax.rem(upper, rows)
-    own_col = lax.rem(lax.div(lower, rows), cols)
-    upper_col = lax.div(lax.rem(upper, cells), rows)
-    away = lax.rem(lower, rows) ^ own_row
-    upper_at = (upper_col ^ own_col) * repeats + lax.div(upper, cells)
-    lower_out = away * repeats + lax.div(lower, cells)
-    lower_at = mirrored_bits(away, rows) * repeats + lax.div(lower, cells)
-    return upper_at, lower_out, lower_at
-
-
-def multiply(count, tiles, held, total, at, contracted):
-    filled = count[0]
-    total[...] = jnp.zeros_like(total)
+def log2(n):
+    return n.bit_length() - 1
+
+
+def gathering(n):
+    return [1 << i for i in reversed(range(log2(n)))]
+
+
+class Places:
+    def __init__(self, coords, rows, cols, repeats):
+        self.coords, self.rows, self.cols, self.repeats = coords, rows, cols, repeats
+        self.cells = log2(rows * cols)
+
+    def away(self, s):
+        return (self.coords[0, s] ^ self.coords[1, s]) & (self.rows - 1)
+
+    def row_block(self, s):
+        upper, lower = self.coords[0, s], self.coords[1, s]
+        across = ((upper >> log2(self.rows)) ^ (lower >> log2(self.rows))) & (self.cols - 1)
+        return across * self.repeats + (upper >> self.cells)
+
+    def column_block(self, s, place):
+        return place * self.repeats + (self.coords[1, s] >> self.cells)
+
+
+def multiply(start, stop, listed, tiles, held, total, at, contracted):
+    slots = tiles.shape[0]
 
     def turn(g, carry):
         for q in range(GROUP):
-            s = g * GROUP + q
+            i = start + g * GROUP + q
+            s = jnp.clip(listed(i), 0, slots - 1)
             source, target = at(s)
             x = held[source]
-            x = jnp.where(s < filled, x, jnp.zeros_like(x))
+            x = jnp.where(i < stop, x, jnp.zeros_like(x))
             total[target] += lax.dot_general(
                 x, tiles[s], (((1,), (contracted,)), ((), ())), preferred_element_type=jnp.float32
             )
         return carry
 
-    lax.fori_loop(0, lax.div(filled + GROUP - 1, GROUP), turn, 0)
+    lax.fori_loop(0, lax.div(stop - start + GROUP - 1, GROUP), turn, 0)
 
 
 def load_pieces(pieces, held):
@@ -92,26 +104,40 @@
 def mirror_kernel(rows, cols, repeats, away, count, coords, tiles, *refs):
     *pieces, total, coded, held = refs
     load_pieces(pieces, held)
+    places = Places(coords, rows, cols, repeats)
+    total[...] = jnp.zeros_like(total)
 
     def at(s):
-        upper_at, lower_out, _ = places(coords, s, rows, cols, repeats)
-        return upper_at, lower_out
-
-    multiply(count, tiles, held, total, at, 0)
+        return places.row_block(s), places.column_block(s, places.away(s))
+
+    multiply(0, count[0], lambda i: i, tiles, held, total, at, 0)
     for i, o in enumerate(away):
         encode([total[o * repeats + k] for k in range(repeats)], coded.at[i])
 
 
-def forward_kernel(rows, cols, repeats, count, coords, tiles, *refs):
-    *refs, held, total = refs
-    pieces, outs = refs[:-cols], refs[-cols:]
+def early_kernel(rows, cols, repeats, splits, lists, coords, tiles, *refs):
+    *pieces, total, held = refs
     load_pieces(pieces, held)
+    places = Places(coords, rows, cols, repeats)
+    total[...] = jnp.zeros_like(total)
 
     def at(s):
-        upper_at, _, lower_at = places(coords, s, rows, cols, repeats)
-        return lower_at, upper_at
-
-    multiply(count, tiles, held, total, at, 1)
+        place = mirrored_bits(places.away(s), rows) & (rows // 2 - 1)
+        return places.column_block(s, place), places.row_block(s)
+
+    multiply(0, splits[0], lambda i: lists[i], tiles, held, total, at, 1)
+
+
+def forward_kernel(rows, cols, repeats, splits, lists, coords, tiles, begun, held, *refs):
+    *outs, total = refs
+    places = Places(coords, rows, cols, repeats)
+    total[...] = begun[...]
+
+    def at(s):
+        place = mirrored_bits(places.away(s), rows) & (rows // 2 - 1)
+        return places.column_block(s, place), places.row_block(s)
+
+    multiply(splits[1], tiles.shape[0], lambda i: lists[i], tiles, held, total, at, 1)
     outs[0][...] = total[0:repeats]
     for o in range(1, cols):
         encode([total[o * repeats + k] for k in range(repeats)], outs[o])
@@ -150,6 +176,25 @@
     copy.wait()
 
 
+def plan_kernel(rows, slots, count, coords, after, splits, lists):
+    late = log2(gathering(rows)[-1])
+    filled = count[0]
+
+    def note(g, ends):
+        front, back = ends
+        for q in range(GROUP):
+            s = g * GROUP + q
+            used = jnp.where(s < filled, 1, 0)
+            away = coords[0, s] ^ coords[1, s]
+            flag = ((away >> late) & used) ^ used
+            spot = jnp.where(flag == 1, front, back - 1)
+            lists[jnp.where(used == 1, spot, slots)] = s
+            front, back = front + flag, back - used + flag
+        return front, back
+
+    splits[0], splits[1] = lax.fori_loop(0, slots // GROUP, note, (0, slots))
+
+
 def halving(n):
     bits = [1 << i for i in reversed(range(n.bit_length() - 1))]
     return bits[1:] + bits[:1]
@@ -180,6 +225,7 @@
         cost_estimate=pl.CostEstimate(flops=1 << 36, bytes_accessed=1 << 10, transcendentals=0),
         name="anchor",
     )()
+    smem = pl.BlockSpec(memory_space=pltpu.SMEM)
     near = pl.pallas_call(
         prepare_kernel,
         out_shape=jax.ShapeDtypeStruct(mine.shape, mine.dtype),
@@ -211,10 +257,9 @@
         column_pieces.append(lax.ppermute(held, "row", partners(rows, bit)))
         bit //= 2
 
-    smem = pl.BlockSpec(memory_space=pltpu.SMEM)
     params = pltpu.CompilerParams(vmem_limit_bytes=16 << 20)
     cost = pl.CostEstimate(
-        flops=2 * slots * vec * width * width, bytes_accessed=2 * slots * width * width, transcendentals=0
+        flops=slots * vec * width * width, bytes_accessed=slots * width * width, transcendentals=0
     )
     small = pl.CostEstimate(flops=0, bytes_accessed=1 << 20, transcendentals=0)
 
@@ -237,6 +282,17 @@
         cost_estimate=cost,
         name="mirror",
     )(filled, coords, mats, *row_pieces)
+
+    splits, lists = pl.pallas_call(
+        functools.partial(plan_kernel, rows, slots),
+        out_shape=[jax.ShapeDtypeStruct((2,), jnp.int32), jax.ShapeDtypeStruct((slots + GROUP,), jnp.int32)],
+        in_specs=[smem, smem, vmem],
+        out_specs=[smem, smem],
+        compiler_params=pltpu.CompilerParams(vmem_limit_bytes=2 << 20),
+        cost_estimate=small,
+        name="plan",
+    )(filled, coords, near)
+    plan = (splits, lists, coords)
     for step, bit in enumerate(order):
         received = lax.ppermute(sent, "row", partners(rows, bit))
         if step == len(order) - 1:
@@ -255,19 +311,26 @@
         )(total, received)
         held = [o for o in left if not o & following]
 
+    begun = pl.pallas_call(
+        functools.partial(early_kernel, rows, cols, repeats),
+        out_shape=blocks(cols),
+        in_specs=[smem] * 3 + [vmem] * len(column_pieces),
+        out_specs=vmem,
+        scratch_shapes=[pltpu.VMEM((rows // 2 * repeats, vec, width), jnp.bfloat16)],
+        compiler_params=params,
+        cost_estimate=cost,
+        name="early",
+    )(*plan, mats, *column_pieces[:-1])
     own, *partial = pl.pallas_call(
         functools.partial(forward_kernel, rows, cols, repeats),
         out_shape=[blocks(1)] + [jax.ShapeDtypeStruct((coded_rows, width), jnp.int16)] * (cols - 1),
-        in_specs=[smem, smem] + [vmem] * (1 + len(column_pieces)),
+        in_specs=[smem] * 3 + [vmem] * 3,
         out_specs=[vmem] * cols,
-        scratch_shapes=[
-            pltpu.VMEM((rows * repeats, vec, width), jnp.bfloat16),
-            pltpu.VMEM((cols * repeats, vec, width), jnp.float32),
-        ],
+        scratch_shapes=[pltpu.VMEM((cols * repeats, vec, width), jnp.float32)],
         compiler_params=params,
         cost_estimate=cost,
         name="forward",
-    )(filled, coords, mats, *column_pieces)
+    )(*plan, mats, begun, column_pieces[-1])
     gathered = []
     for o, part in enumerate(partial):
         gathered.append(lax.ppermute(part, "col", partners(cols, o + 1)))

time: 32.3 us -> 34.9 us (1.080)
  Pallas kernels: 4.44 us -> 6.51 us
  waiting for transfers between devices: 8.25 us -> 9.13 us
    pallas_call x0 -> x2, Pallas kernels: none -> 2.8 us  [the longest x1 1.56 us: body(): pl.pallas_call(functools.partial(plan_kernel, rows, slots), out_shape=[ja...]
    ppermute x3, starting transfers between devices: 6.11 us -> 5.12 us  [body(): received = lax.ppermute(sent, 'row', partners(rows, bit))]
    ppermute x3, waiting for transfers between devices: 5.64 us -> 6.52 us  [body(): received = lax.ppermute(sent, 'row', partners(rows, bit))]
    ppermute x3, starting transfers between devices: 2.38 us -> 3.1 us  [body(): gathered.append(lax.ppermute(part, 'col', partners(cols, o + 1)))]
    pallas_call x1, Pallas kernels: 2 us -> 1.34 us  [body(): pl.pallas_call(functools.partial(forward_kernel, rows, cols, repeats), ou...]
  transfers between devices with their start and end apart: 12 -> 12, of which waited for: 4 -> 4; matrix products, arithmetic and copies ran while one was open for 0% -> 0% of each run, Pallas kernels for 12% -> 17%
where the time goes in v1:
time: 34.9 us; the launch traced here: 34.8 us
  starting transfers between devices  18.4 us (53%)
  waiting for transfers between devices  9.13 us (26%)
  Pallas kernels  6.51 us (19%)
  between operations  0.72 us (2%)
    ppermute x3, starting transfers between devices, body(): column_pieces.append(lax.ppermute(held, 'row', partners(rows, bit)))  6.57 us
    ppermute x3, waiting for transfers between devices, body(): received = lax.ppermute(sent, 'row', partners(rows, bit))  6.52 us
    ppermute x3, starting transfers between devices, body(): received = lax.ppermute(sent, 'row', partners(rows, bit))  5.12 us
    ppermute x3, starting transfers between devices, body(): moved.append(lax.ppermute(piece, 'col', partners(cols, bit)))  3.58 us
    ppermute x3, starting transfers between devices, body(): gathered.append(lax.ppermute(part, 'col', partners(cols, o + 1)))  3.1 us
    ppermute x3, waiting for transfers between devices, body(): column_pieces.append(lax.ppermute(held, 'row', partners(rows, bit)))  2.4 us
    pallas_call x1, Pallas kernels, body(): pl.pallas_call(functools.partial(plan_kernel, rows, slots), out_shape=[ja...  1.56 us
    pallas_call x1, Pallas kernels, body(): pl.pallas_call(functools.partial(mirror_kernel, rows, cols, repeats, away...  1.49 us
  transfers between devices with their start and end apart: 12, of which 4 were waited for; matrix products, arithmetic and copies ran while one was open for 0% of the time, Pallas kernels for 17%

profile of v1, /device:TPU:0, one launch (start us, length us, event | category | flops | bytes accessed | tf_op | source)
XLA Modules:
  0.0 34.8 jit_solution(989319331071837542)
XLA Ops:
  0.0 3.1 %collective-permute-start.1 = (bf16[4,16,256]{2,1,0:T(8,128)(2,1)}, bf16[4,16,256]{2,1,0:T(8,128)(2,1)S(1)}, u32[]{:S(2)}, u32[]{:S(2)}) collective-permute-start(bf16[4,16,256]{2,1,0:T(8,128)(2,1)} %bitcast.18), channel_id=1, source_target_pairs={{0,2},{1,3},{2,0},{3,1},{4,6},{5,7},{6,4},{7,5},{8,10},{9,11},{10,... | collective-permute-start | bytes 98312 | tf_op jit(solution)/shard_map/ppermute | solution.py:246
  3.1 2.6 %collective-permute-start.5 = (bf16[4,16,256]{2,1,0:T(8,128)(2,1)}, bf16[4,16,256]{2,1,0:T(8,128)(2,1)S(1)}, u32[]{:S(2)}, u32[]{:S(2)}) collective-permute-start(bf16[4,16,256]{2,1,0:T(8,128)(2,1)} %bitcast.19), channel_id=1, source_target_pairs={{0,16},{4,20},{8,24},{12,28},{16,0},{20,4},{24,8},{28,12},{1,17},{... | collective-permute-start | bytes 98312 | tf_op jit(solution)/shard_map/ppermute | solution.py:257
  5.7 0.0 copy-done
  5.7 2.4 %collective-permute-done.5.refs_1_ = bf16[4,16,256]{2,1,0:T(8,128)(2,1)S(1)} collective-permute-done((bf16[4,16,256]{2,1,0:T(8,128)(2,1)}, bf16[4,16,256]{2,1,0:T(8,128)(2,1)S(1)}, u32[]{:S(2)}, u32[]{:S(2)}) %collective-permute-start.5) | collective-permute-done | bytes 32800 | tf_op jit(solution)/shard_map/ppermute | solution.py:257
  8.1 1.6 %collective-permute-start.6 = (bf16[8,16,256]{2,1,0:T(8,128)(2,1)S(1)}, bf16[8,16,256]{2,1,0:T(8,128)(2,1)S(1)}, u32[]{:S(2)}, u32[]{:S(2)}) collective-permute-start(bf16[8,16,256]{2,1,0:T(8,128)(2,1)S(1)} %pad_maximum_fusion.1), channel_id=1, source_target_pairs={{0,8},{4,12},{8,0},{12,4},{16,24},{20,28},{24,16},{28,20},{1,9},{5... | collective-permute-start | bytes 196616 | tf_op jit(solution)/shard_map/ppermute | solution.py:257
  9.8 0.0 collective-permute-start
  9.8 0.0 collective-permute-done.1.refs_2_
  9.8 0.5 %collective-permute-start.2 = (bf16[4,16,256]{2,1,0:T(8,128)(2,1)S(1)}, bf16[4,16,256]{2,1,0:T(8,128)(2,1)S(1)}, u32[]{:S(2)}, u32[]{:S(2)}) collective-permute-start(bf16[4,16,256]{2,1,0:T(8,128)(2,1)S(1)} %collective-permute-done.1.refs_2_), channel_id=1, source_target_pairs={{0,1},{1,0},{2,3},{3,2},{4,5},{5,4},{6,7},{7,6},{8,9},{9,8},{10,11... | collective-permute-start | bytes 98312 | tf_op jit(solution)/shard_map/ppermute | solution.py:246
  10.9 0.0 collective-permute-done.refs_1_
  11.0 0.2 collective-permute-done.2.refs_3_
  11.1 1.5 %mirror.1 = (f32[32,16,256]{2,1,0:T(8,128)S(1)}, s16[4,72,256]{2,1,0:T(8,128)(2,1)S(1)}) custom-call(s32[1]{0:T(128)} %bitcast.10.count, s32[2,64]{1,0:T(2,128)S(1)} %bitcast.22, bf16[64,256,256]{2,1,0:T(8,128)(2,1)S(1)} %bitcast.14, bf16[4,16,256]{2,1,0:T(8,128)(2,1)S(1)} %prepare.1.refs_0_.after, bf16[4,16,256]{2,1,0:T(8,128)(2,1)S(1)} %collective-permute-done.refs_1_, ...), custom_call_target="tpu_custom_call" | custom-call | flops 67108864 | bytes 4194304 | tf_op jit(solution)/shard_map/mirror/pallas_call | solution.py:275
  12.6 0.5 %collective-permute-start.3 = (s16[4,72,256]{2,1,0:T(8,128)(2,1)S(1)}, s16[4,72,256]{2,1,0:T(8,128)(2,1)S(1)}, u32[]{:S(2)}, u32[]{:S(2)}) collective-permute-start(s16[4,72,256]{2,1,0:T(8,128)(2,1)S(1)} %get-tuple-element.18), channel_id=1, source_target_pairs={{0,8},{4,12},{8,0},{12,4},{16,24},{20,28},{24,16},{28,20},{1,9},{5... | collective-permute-start | bytes 442376 | tf_op jit(solution)/shard_map/ppermute | solution.py:297
  13.2 0.0 collective-permute-done.6.refs_2_
  13.2 2.3 %collective-permute-start.7 = (bf16[16,16,256]{2,1,0:T(8,128)(2,1)S(1)}, bf16[16,16,256]{2,1,0:T(8,128)(2,1)S(1)}, u32[]{:S(2)}, u32[]{:S(2)}) collective-permute-start(bf16[16,16,256]{2,1,0:T(8,128)(2,1)S(1)} %pad_maximum_fusion), channel_id=1, source_target_pairs={{0,4},{4,0},{8,12},{12,8},{16,20},{20,16},{24,28},{28,24},{1,5},{5... | collective-permute-start | bytes 393224 | tf_op jit(solution)/shard_map/ppermute | solution.py:257
  15.5 3.7 %collective-permute-done.3.received = s16[4,72,256]{2,1,0:T(8,128)(2,1)S(1)} collective-permute-done((s16[4,72,256]{2,1,0:T(8,128)(2,1)S(1)}, s16[4,72,256]{2,1,0:T(8,128)(2,1)S(1)}, u32[]{:S(2)}, u32[]{:S(2)}) %collective-permute-start.3) | collective-permute-done | bytes 147488 | tf_op jit(solution)/shard_map/ppermute | solution.py:297
  19.2 0.1 shard_map.46
  19.4 1.5 %collective-permute-start.4 = (s16[2,72,256]{2,1,0:T(8,128)(2,1)S(1)}, s16[2,72,256]{2,1,0:T(8,128)(2,1)S(1)}, u32[]{:S(2)}, u32[]{:S(2)}) collective-permute-start(s16[2,72,256]{2,1,0:T(8,128)(2,1)S(1)} %get-tuple-element.20), channel_id=1, source_target_pairs={{0,4},{4,0},{8,12},{12,8},{16,20},{20,16},{24,28},{28,24},{1,5},{5... | collective-permute-start | bytes 221192 | tf_op jit(solution)/shard_map/ppermute | solution.py:297
  20.9 1.6 %plan.1 = (s32[2]{0:T(128)S(1)}, s32[80]{0:T(128)S(1)}) custom-call(s32[1]{0:T(128)} %bitcast.11.count, s32[2,64]{1,0:T(2,128)S(1)} %bitcast.23, bf16[4,16,256]{2,1,0:T(8,128)(2,1)S(1)} %prepare.1.refs_0_.after), custom_call_target="tpu_custom_call" | custom-call | bytes 1048576 | tf_op jit(solution)/shard_map/plan/pallas_call | solution.py:286
  22.4 1.2 %early.1.begun = f32[16,16,256]{2,1,0:T(8,128)S(1)} custom-call(s32[2]{0:T(128)S(1)} %get-tuple-element.22.splits, s32[80]{0:T(128)S(1)} %get-tuple-element.23.lists, s32[2,64]{1,0:T(2,128)S(1)} %bitcast.24, bf16[64,256,256]{2,1,0:T(8,128)(2,1)S(1)} %bitcast.15, bf16[4,16,256]{2,1,0:T(8,128)(2,1)S(1)} %prepare.1.refs_0_.after, ...), custom_call_target="tpu_custom_call" | custom-call | flops 67108864 | bytes 4194304 | tf_op jit(solution)/shard_map/early/pallas_call | solution.py:314
  23.7 0.0 collective-permute-done.7.held
  23.7 1.3 %forward.1 = (f32[4,16,256]{2,1,0:T(8,128)S(1)}, s16[72,256]{1,0:T(8,128)(2,1)S(1)}, s16[72,256]{1,0:T(8,128)(2,1)S(1)}, s16[72,256]{1,0:T(8,128)(2,1)S(1)}) custom-call(s32[2]{0:T(128)S(1)} %get-tuple-element.22.splits, s32[80]{0:T(128)S(1)} %get-tuple-element.23.lists, s32[2,64]{1,0:T(2,128)S(1)} %bitcast.25, bf16[64,256,256]{2,1,0:T(8,128)(2,1)S(1)} %bitcast.16, ...), custom_call_target="tpu_custom_call" | custom-call | flops 67108864 | bytes 4194304 | tf_op jit(solution)/shard_map/forward/pallas_call | solution.py:324
  25.0 1.7 %collective-permute-start.9 = (s16[72,256]{1,0:T(8,128)(2,1)S(1)}, s16[72,256]{1,0:T(8,128)(2,1)S(1)}, u32[]{:S(2)}, u32[]{:S(2)}) collective-permute-start(s16[72,256]{1,0:T(8,128)(2,1)S(1)} %get-tuple-element.26), channel_id=1, source_target_pairs={{0,1},{1,0},{2,3},{3,2},{4,5},{5,4},{6,7},{7,6},{8,9},{9,8},{10,11... | collective-permute-start | bytes 110600 | tf_op jit(solution)/shard_map/ppermute | solution.py:336
  26.7 0.0 collective-permute-start.10
  26.7 1.4 %collective-permute-start.11 = (s16[72,256]{1,0:T(8,128)(2,1)S(1)}, s16[72,256]{1,0:T(8,128)(2,1)S(1)}, u32[]{:S(2)}, u32[]{:S(2)}) collective-permute-start(s16[72,256]{1,0:T(8,128)(2,1)S(1)} %get-tuple-element.28), channel_id=1, source_target_pairs={{0,3},{1,2},{2,1},{3,0},{4,7},{5,6},{6,5},{7,4},{8,11},{9,10},{10,... | collective-permute-start | bytes 110600 | tf_op jit(solution)/shard_map/ppermute | solution.py:336
  28.1 0.0 collective-permute-done.4.received
  28.1 0.1 shard_map.47
  28.2 3.1 %collective-permute-start.8 = (s16[1,72,256]{2,1,0:T(8,128)(2,1)S(1)}, s16[1,72,256]{2,1,0:T(8,128)(2,1)S(1)}, u32[]{:S(2)}, u32[]{:S(2)}) collective-permute-start(s16[1,72,256]{2,1,0:T(8,128)(2,1)S(1)} %get-tuple-element.25), channel_id=1, source_target_pairs={{0,16},{4,20},{8,24},{12,28},{16,0},{20,4},{24,8},{28,12},{1,17},{... | collective-permute-start | bytes 110600 | tf_op jit(solution)/shard_map/ppermute | solution.py:297
  31.3 0.0 collective-permute-done.9.refs_1_
  31.3 0.0 collective-permute-done.10.refs_2_
  31.3 0.0 collective-permute-done.11.refs_3_
  31.3 2.8 %collective-permute-done.8 = s16[1,72,256]{2,1,0:T(8,128)(2,1)S(1)} collective-permute-done((s16[1,72,256]{2,1,0:T(8,128)(2,1)S(1)}, s16[1,72,256]{2,1,0:T(8,128)(2,1)S(1)}, u32[]{:S(2)}, u32[]{:S(2)}) %collective-permute-start.8) | collective-permute-done | bytes 36896 | tf_op jit(solution)/shard_map/ppermute | solution.py:297
  34.1 0.7 %final.1 = f32[4,16,256]{2,1,0:T(8,128)} custom-call(f32[4,16,256]{2,1,0:T(8,128)S(1)} %get-tuple-element.21.own_rows, f32[4,16,256]{2,1,0:T(8,128)S(1)} %get-tuple-element.24.own_cols, s16[72,256]{1,0:T(8,128)(2,1)S(1)} %bitcast.17, s16[72,256]{1,0:T(8,128)(2,1)S(1)} %collective-permute-done.9.refs_1_, s16[72,256]{1,0:T(8,128)(2,1)S(1)} %collective-permute-done.10.refs_2_, ...), custom_call_target="tpu_custom_call" | custom-call | tf_op jit(solution)/shard_map/final/pallas_call | solution.py:338
  (12 shorter events, 0.1 us)
Async XLA Ops:
  0.0 11.1 %slice-start = ((s8[8388608]{0:T(1024)(128)(4,1)}), s8[4194304]{0:T(1024)(128)(4,1)S(1)}, s32[]{:S(2)}) async-start(s8[8388608]{0:T(1024)(128)(4,1)} %bitcast.12), calls=%async_computation | async-start | bytes 8388608
  0.0 5.7 %copy-start = (bf16[4,1,1,16,256]{4,3,2,1,0:T(8,128)(2,1)S(1)}, bf16[4,1,1,16,256]{4,3,2,1,0:T(8,128)(2,1)}, u32[]{:S(2)}) copy-start(bf16[4,1,1,16,256]{4,3,2,1,0:T(8,128)(2,1)} %param.4) | copy-start | bytes 98308
  0.0 11.1 %slice-start.1 = ((s8[8388608]{0:T(1024)(128)(4,1)}), s8[4194304]{0:T(1024)(128)(4,1)S(1)}, s32[]{:S(2)}) async-start(s8[8388608]{0:T(1024)(128)(4,1)} %bitcast.12), calls=%async_computation.1 | async-start | bytes 8388608
  0.0 11.1 %copy-start.1 = (s32[1,1,64,2]{2,3,1,0:T(2,128)S(1)}, s32[1,1,64,2]{2,3,1,0:T(2,128)}, u32[]{:S(2)}) copy-start(s32[1,1,64,2]{2,3,1,0:T(2,128)} %param.6) | copy-start | bytes 1540
  0.0 9.8 %collective-permute-start.1 = (bf16[4,16,256]{2,1,0:T(8,128)(2,1)}, bf16[4,16,256]{2,1,0:T(8,128)(2,1)S(1)}, u32[]{:S(2)}, u32[]{:S(2)}) collective-permute-start(bf16[4,16,256]{2,1,0:T(8,128)(2,1)} %bitcast.18), channel_id=1, source_target_pairs={{0,2},{1,3},{2,0},{3,1},{4,6},{5,7},{6,4},{7,5},{8,10},{9,11},{10,... | collective-permute-start | bytes 98312 | tf_op jit(solution)/shard_map/ppermute | solution.py:246
  3.1 5.0 %collective-permute-start.5 = (bf16[4,16,256]{2,1,0:T(8,128)(2,1)}, bf16[4,16,256]{2,1,0:T(8,128)(2,1)S(1)}, u32[]{:S(2)}, u32[]{:S(2)}) collective-permute-start(bf16[4,16,256]{2,1,0:T(8,128)(2,1)} %bitcast.19), channel_id=1, source_target_pairs={{0,16},{4,20},{8,24},{12,28},{16,0},{20,4},{24,8},{28,12},{1,17},{... | collective-permute-start | bytes 98312 | tf_op jit(solution)/shard_map/ppermute | solution.py:257
  8.1 5.0 %collective-permute-start.6 = (bf16[8,16,256]{2,1,0:T(8,128)(2,1)S(1)}, bf16[8,16,256]{2,1,0:T(8,128)(2,1)S(1)}, u32[]{:S(2)}, u32[]{:S(2)}) collective-permute-start(bf16[8,16,256]{2,1,0:T(8,128)(2,1)S(1)} %pad_maximum_fusion.1), channel_id=1, source_target_pairs={{0,8},{4,12},{8,0},{12,4},{16,24},{20,28},{24,16},{28,20},{1,9},{5... | collective-permute-start | bytes 196616 | tf_op jit(solution)/shard_map/ppermute | solution.py:257
  9.8 1.2 %collective-permute-start = (bf16[4,16,256]{2,1,0:T(8,128)(2,1)S(1)}, bf16[4,16,256]{2,1,0:T(8,128)(2,1)S(1)}, u32[]{:S(2)}, u32[]{:S(2)}) collective-permute-start(bf16[4,16,256]{2,1,0:T(8,128)(2,1)S(1)} %bitcast.21), channel_id=1, source_target_pairs={{0,1},{1,0},{2,3},{3,2},{4,5},{5,4},{6,7},{7,6},{8,9},{9,8},{10,11... | collective-permute-start | bytes 98312 | tf_op jit(solution)/shard_map/ppermute | solution.py:246
  9.8 1.4 %collective-permute-start.2 = (bf16[4,16,256]{2,1,0:T(8,128)(2,1)S(1)}, bf16[4,16,256]{2,1,0:T(8,128)(2,1)S(1)}, u32[]{:S(2)}, u32[]{:S(2)}) collective-permute-start(bf16[4,16,256]{2,1,0:T(8,128)(2,1)S(1)} %collective-permute-done.1.refs_2_), channel_id=1, source_target_pairs={{0,1},{1,0},{2,3},{3,2},{4,5},{5,4},{6,7},{7,6},{8,9},{9,8},{10,11... | collective-permute-start | bytes 98312 | tf_op jit(solution)/shard_map/ppermute | solution.py:246
  12.6 6.6 %collective-permute-start.3 = (s16[4,72,256]{2,1,0:T(8,128)(2,1)S(1)}, s16[4,72,256]{2,1,0:T(8,128)(2,1)S(1)}, u32[]{:S(2)}, u32[]{:S(2)}) collective-permute-start(s16[4,72,256]{2,1,0:T(8,128)(2,1)S(1)} %get-tuple-element.18), channel_id=1, source_target_pairs={{0,8},{4,12},{8,0},{12,4},{16,24},{20,28},{24,16},{28,20},{1,9},{5... | collective-permute-start | bytes 442376 | tf_op jit(solution)/shard_map/ppermute | solution.py:297
  13.2 10.5 %collective-permute-start.7 = (bf16[16,16,256]{2,1,0:T(8,128)(2,1)S(1)}, bf16[16,16,256]{2,1,0:T(8,128)(2,1)S(1)}, u32[]{:S(2)}, u32[]{:S(2)}) collective-permute-start(bf16[16,16,256]{2,1,0:T(8,128)(2,1)S(1)} %pad_maximum_fusion), channel_id=1, source_target_pairs={{0,4},{4,0},{8,12},{12,8},{16,20},{20,16},{24,28},{28,24},{1,5},{5... | collective-permute-start | bytes 393224 | tf_op jit(solution)/shard_map/ppermute | solution.py:257
  19.4 8.8 %collective-permute-start.4 = (s16[2,72,256]{2,1,0:T(8,128)(2,1)S(1)}, s16[2,72,256]{2,1,0:T(8,128)(2,1)S(1)}, u32[]{:S(2)}, u32[]{:S(2)}) collective-permute-start(s16[2,72,256]{2,1,0:T(8,128)(2,1)S(1)} %get-tuple-element.20), channel_id=1, source_target_pairs={{0,4},{4,0},{8,12},{12,8},{16,20},{20,16},{24,28},{28,24},{1,5},{5... | collective-permute-start | bytes 221192 | tf_op jit(solution)/shard_map/ppermute | solution.py:297
  25.0 6.3 %collective-permute-start.9 = (s16[72,256]{1,0:T(8,128)(2,1)S(1)}, s16[72,256]{1,0:T(8,128)(2,1)S(1)}, u32[]{:S(2)}, u32[]{:S(2)}) collective-permute-start(s16[72,256]{1,0:T(8,128)(2,1)S(1)} %get-tuple-element.26), channel_id=1, source_target_pairs={{0,1},{1,0},{2,3},{3,2},{4,5},{5,4},{6,7},{7,6},{8,9},{9,8},{10,11... | collective-permute-start | bytes 110600 | tf_op jit(solution)/shard_map/ppermute | solution.py:336
  26.7 4.6 %collective-permute-start.10 = (s16[72,256]{1,0:T(8,128)(2,1)S(1)}, s16[72,256]{1,0:T(8,128)(2,1)S(1)}, u32[]{:S(2)}, u32[]{:S(2)}) collective-permute-start(s16[72,256]{1,0:T(8,128)(2,1)S(1)} %get-tuple-element.27), channel_id=1, source_target_pairs={{0,2},{1,3},{2,0},{3,1},{4,6},{5,7},{6,4},{7,5},{8,10},{9,11},{10,... | collective-permute-start | bytes 110600 | tf_op jit(solution)/shard_map/ppermute | solution.py:336
  26.7 4.6 %collective-permute-start.11 = (s16[72,256]{1,0:T(8,128)(2,1)S(1)}, s16[72,256]{1,0:T(8,128)(2,1)S(1)}, u32[]{:S(2)}, u32[]{:S(2)}) collective-permute-start(s16[72,256]{1,0:T(8,128)(2,1)S(1)} %get-tuple-element.28), channel_id=1, source_target_pairs={{0,3},{1,2},{2,1},{3,0},{4,7},{5,6},{6,5},{7,4},{8,11},{9,10},{10,... | collective-permute-start | bytes 110600 | tf_op jit(solution)/shard_map/ppermute | solution.py:336
  28.2 5.9 %collective-permute-start.8 = (s16[1,72,256]{2,1,0:T(8,128)(2,1)S(1)}, s16[1,72,256]{2,1,0:T(8,128)(2,1)S(1)}, u32[]{:S(2)}, u32[]{:S(2)}) collective-permute-start(s16[1,72,256]{2,1,0:T(8,128)(2,1)S(1)} %get-tuple-element.25), channel_id=1, source_target_pairs={{0,16},{4,20},{8,24},{12,28},{16,0},{20,4},{24,8},{28,12},{1,17},{... | collective-permute-start | bytes 110600 | tf_op jit(solution)/shard_map/ppermute | solution.py:297
